TPU v7x, 256 devices: a whole 4x4x8 slice. The times are simulated.
256 devices in a mesh: row: 32 (over z, y), col: 8 (over x, core).
Axes of the slice: x: 4, y: 4, z: 8, core: 2. Of those that a mesh axis runs over, the one named last changes fastest.
Arguments:
- feats: bfloat16 [131072, 256], P(('row', 'col')), may hold values from -6 to 6
- w_msg: bfloat16 [256, 256], replicated, may hold values from -0.375 to 0.375
- w_self: bfloat16 [256, 256], replicated, may hold values from -0.375 to 0.375
- bias: float32 [256], replicated, may hold values from -3 to 3
- hit_mask: int32 [131072], P(('row', 'col')), may hold values 0 or 1
- block_cols: int32 [32, 8, 96], P('row', 'col'), may hold values from 0 to 127, as said below
- block_count: int32 [32, 8], P('row', 'col'), may hold values from 32 to 96, as said below
- edge_vals: bfloat16 [32, 8, 96, 128, 128], P('row', 'col'), may hold values from -0.125 to 0.125
- grad_out: bfloat16 [131072, 256], P(('row', 'col')), may hold values from -3 to 3
Outputs:
- hidden: bfloat16 [131072, 256], P(('row', 'col'))
- grad_feats: bfloat16 [131072, 256], P(('row', 'col'))
- edge_grad: bfloat16 [32, 8, 96, 128, 128], P('row', 'col')
- w_msg_grad: float32 [256, 256], replicated
- w_self_grad: float32 [256, 256], replicated
- bias_grad: float32 [256], replicated
Inputs may be any that keep to these rules, and one draw needn't show every extreme that they name: `block_cols`: slot s of a tile serves the tile's local block row s % 32; the block columns of the slots that serve one block row of one tile are different. Slots from block_count on are unused.
All inputs are finite; a program needn't handle non-finite values. No bound on the sum of `hit_mask` on one device may be relied on, other than what follows from the above.
Results may differ from a plain program's by a relative error of at most 0.015.
Values may be sent and summed in bfloat16 or wider, within the bound.
A program may use at most 128 MiB of HBM per device.

v0:
```python
import math
import jax
import jax.numpy as jnp
from jax import lax
from jax.sharding import PartitionSpec as P


def activate(pre, row_mask, grad_in):
    sig = jax.nn.sigmoid(pre)
    hidden = (pre * sig * row_mask).astype(jnp.bfloat16)
    deriv = sig * (1.0 + pre * (1.0 - sig))
    grad_pre = (grad_in.astype(jnp.float32) * row_mask * deriv).astype(jnp.bfloat16)
    return (hidden, grad_pre)


def per_device(feats, w_msg, w_self, bias, hit_mask, block_cols, block_count, edge_vals, grad_out):
    row_count = lax.axis_size("row")
    col_count = lax.axis_size("col")
    own_rows = feats.shape[0]
    width = feats.shape[1]
    row_mask = hit_mask.astype(jnp.float32)[:, None]
    messages = (jnp.dot(feats, w_msg, preferred_element_type=jnp.float32) * row_mask).astype(
        jnp.bfloat16
    )
    column_msgs = lax.all_gather(messages, "row", axis=0, tiled=True)
    slot_cols = block_cols[0, 0]
    edge_block = edge_vals[0, 0]
    slot_total = edge_block.shape[0]
    edge_size = edge_block.shape[1]
    tile_rows = col_count * own_rows // edge_size
    tile_cols = row_count * own_rows // edge_size
    slot_depth = slot_total // tile_rows
    slot_flags = jnp.arange(slot_total, dtype=jnp.int32) < block_count[0, 0]
    edge_live = (edge_block * slot_flags.astype(jnp.bfloat16)[:, None, None]).reshape(
        slot_depth, tile_rows, edge_size, edge_size
    )
    col_blocks = column_msgs.reshape(tile_cols, edge_size, width)[slot_cols].reshape(
        slot_depth, tile_rows, edge_size, width
    )
    partial_value = jnp.einsum(
        "krij,krjf->rif", edge_live, col_blocks, preferred_element_type=jnp.float32
    ).reshape(tile_rows * edge_size, width)
    summed = lax.psum_scatter(
        partial_value.astype(jnp.bfloat16), "col", scatter_dimension=0, tiled=True
    ).astype(jnp.float32)
    pre = summed + jnp.dot(feats, w_self, preferred_element_type=jnp.float32) + bias
    hidden, grad_pre = activate(pre, row_mask, grad_out)
    grad_rows_all = lax.all_gather(grad_pre, "col", axis=0, tiled=True)
    grad_tile = grad_rows_all.reshape(tile_rows, edge_size, width)
    backward = jnp.einsum(
        "krij,rif->krjf", edge_live, grad_tile, preferred_element_type=jnp.float32
    ).reshape(slot_total, edge_size, width)
    back_part = jax.ops.segment_sum(backward, slot_cols, num_segments=tile_cols).reshape(
        tile_cols * edge_size, width
    )
    edge_grad = (
        jnp.einsum(
            "rif,krjf->krij", grad_tile, col_blocks, preferred_element_type=jnp.float32
        ).reshape(slot_total, edge_size, edge_size)
        * slot_flags.astype(jnp.float32)[:, None, None]
    ).astype(jnp.bfloat16)
    grad_sum = lax.psum_scatter(
        back_part.astype(jnp.bfloat16), "row", scatter_dimension=0, tiled=True
    ).astype(jnp.float32)
    grad_msg = (grad_sum * row_mask).astype(jnp.bfloat16)
    grad_feats = (
        jnp.einsum("hg,fg->hf", grad_msg, w_msg, preferred_element_type=jnp.float32)
        + jnp.einsum("hg,fg->hf", grad_pre, w_self, preferred_element_type=jnp.float32)
    ).astype(jnp.bfloat16)
    local_msg = jnp.einsum("hf,hg->fg", feats, grad_msg, preferred_element_type=jnp.float32)
    local_self = jnp.einsum("hf,hg->fg", feats, grad_pre, preferred_element_type=jnp.float32)
    local_bias = jnp.sum(grad_pre.astype(jnp.float32), axis=0)
    total_msg, total_self, total_bias = lax.psum(
        (local_msg, local_self, local_bias), ("row", "col")
    )
    factor = 1.0 / math.sqrt(own_rows * row_count * col_count)
    return (
        hidden,
        grad_feats,
        edge_grad[None, None],
        total_msg * factor,
        total_self * factor,
        total_bias * factor,
    )


def solution(mesh):
    placed = (
        P(("row", "col"), None),
        P(),
        P(),
        P(),
        P(("row", "col")),
        P("row", "col", None),
        P("row", "col"),
        P("row", "col", None, None, None),
        P(("row", "col"), None),
    )
    return jax.shard_map(
        per_device,
        mesh=mesh,
        in_specs=placed,
        out_specs=(
            P(("row", "col"), None),
            P(("row", "col"), None),
            P("row", "col", None, None, None),
            P(),
            P(),
            P(),
        ),
        check_vma=False,
    )
```

profile of v0, /device:TPU:2, one launch (start us, length us, event | category | flops | bytes accessed | tf_op | source)
XLA Modules:
  0.0 757.9 jit_solution(17679265204071514697)
XLA Ops:
  7.2 0.0 copy-start
  7.2 0.0 all-gather.3.cloned.1.call-start
  7.2 0.7 convert_element_type.67
  7.9 0.2 copy-done
  8.1 1.8 fusion.12
  10.0 0.0 all-gather.3.cloned.1.call-update
  10.0 0.0 reduce-scatter.3.cloned.1.call-start
  10.7 0.7 fusion.16
  11.4 100.7 %all-gather.3.cloned.1.call-done = bf16[16384,256]{1,0:T(8,128)(2,1)} async-done(((bf16[512,256]{1,0:T(8,128)(2,1)}), bf16[16384,256]{1,0:T(8,128)(2,1)}) %all-gather.3.cloned.1.call-update) | async-done | bytes 8388624 | tf_op jit(solution)/shard_map/all_gather | solution.py:25
  112.0 0.0 copy-start.2
  112.0 9.5 %gather_fusion = bf16[96,128,256]{2,1,0:T(8,128)(2,1)} fusion(bf16[128,128,256]{2,1,0:T(8,128)(2,1)} %bitcast.53, s32[1024]{0:T(1024)S(1)} %pad_clamp_fusion), kind=kCustom, calls=%fused_computation | custom fusion | bytes 12583296 | tf_op jit(solution)/shard_map/gather | solution.py:37
  121.5 0.0 copy-done.2
  121.5 0.0 copy-start.5
  121.5 5.5 bitcast_convert_fusion
  127.0 0.0 reduce-scatter.3.cloned.1.call-update
  127.0 0.0 all-gather.5.cloned.1.call-start
  127.1 30.4 %reduce-scatter.3.cloned.1.call-done = bf16[512,256]{1,0:T(8,128)(2,1)} async-done(((bf16[4096,256]{1,0:T(8,128)(2,1)}), bf16[512,256]{1,0:T(8,128)(2,1)}) %reduce-scatter.3.cloned.1.call-update) | async-done | bytes 262160 | tf_op jit(solution)/shard_map/reduce_scatter | solution.py:43
  157.5 0.0 copy-done.5
  157.5 2.3 convert_reduce_fusion
  159.8 0.0 all-gather.5.cloned.1.call-update
  159.8 0.0 reduce-scatter.5.cloned.1.call-start
  159.9 28.7 %all-gather.5.cloned.1.call-done = bf16[4096,256]{1,0:T(8,128)(2,1)} async-done(((bf16[512,256]{1,0:T(8,128)(2,1)}), bf16[4096,256]{1,0:T(8,128)(2,1)}) %all-gather.5.cloned.1.call-update) | async-done | bytes 2097168 | tf_op jit(solution)/shard_map/all_gather | solution.py:48
  188.6 8.0 %convolution_bitcast_fusion = f32[3,32,128,256]{2,3,0,1:T(8,128)} fusion(bf16[32,128,256,1]{2,1,3,0:T(8,128)(2,1)} %bitcast.51, bf16[3,32,128,128]{3,2,1,0:T(8,128)(2,1)S(1)} %bitcast.55, bf16[3,32]{0,1:T(8,128)(2,1)S(1)} %fusion.15), kind=kOutput, calls=%fused_computation.7 | convolution fusion | flops 811597824 | bytes 17825984 | tf_op jit(solution)/shard_map/krij,rif->krjf/dot_general | solution.py:50
  196.6 12.6 %copy.22 = f32[3,32,128,256]{3,2,1,0:T(8,128)} copy(f32[3,32,128,256]{2,3,0,1:T(8,128)} %convolution_bitcast_fusion) | data formatting | bytes 25165824 | tf_op jit(solution)/shard_map/krij,rif->krjf/transpose | solution.py:50
  209.2 7.8 %broadcast_in_dim.2 = f32[128,128,256]{2,1,0:T(8,128)} broadcast(f32[]{:T(128)} %constant.4.clone.1), dimensions={} | broadcast | bytes 16777220 | tf_op jit(solution)/shard_map/broadcast_in_dim | solution.py:53
  217.0 0.0 copy-done.6
  217.0 29.1 %scatter_fusion = f32[128,128,256]{2,1,0:T(8,128)} fusion(f32[128,128,256]{2,1,0:T(8,128)} %broadcast_in_dim.2, s32[96]{0:T(128)S(1)} %bitcast.57, f32[96,128,256]{2,1,0:T(8,128)} %bitcast.46), kind=kCustom, calls=%fused_computation.1 | custom fusion | flops 3145728 | bytes 37749120 | tf_op jit(solution)/shard_map/scatter-add | solution.py:53
  246.1 9.0 %convert_element_type.75 = bf16[128,128,256]{2,1,0:T(8,128)(2,1)} convert(f32[128,128,256]{2,1,0:T(8,128)} %scatter_fusion) | non-fusion elementwise | flops 4194304 | bytes 25165824 | tf_op jit(solution)/shard_map/convert_element_type | solution.py:63
  255.1 0.0 reduce-scatter.5.cloned.1.call-update
  255.2 0.0 all-reduce.3.cloned.1.call-start
  255.2 78.1 %psum.23 = f32[256]{0:T(256)S(1)} all-reduce(f32[256]{0:T(256)S(1)} %get-tuple-element.20), channel_id=1, replica_groups=mesh['row'=32,'col'=8] {'row','col'}, use_global_device_ids=true, to_apply=%region_6.0 | all-reduce | flops 256 | bytes 2048 | tf_op jit(solution)/shard_map/psum | solution.py:73
  333.3 0.6 broadcast_multiply_fusion.2
  333.9 0.0 copy-done.3
  333.9 1.0 convolution_bitcast_fusion.1
  334.9 0.0 copy-done.1
  334.9 7.3 fusion.4
  342.1 6.6 copy.24
  348.7 5.1 multiply_convert_fusion
  353.8 134.4 %reduce-scatter.5.cloned.1.call-done = bf16[512,256]{1,0:T(8,128)(2,1)} async-done(((bf16[16384,256]{1,0:T(8,128)(2,1)}), bf16[512,256]{1,0:T(8,128)(2,1)}) %reduce-scatter.5.cloned.1.call-update) | async-done | bytes 262160 | tf_op jit(solution)/shard_map/reduce_scatter | solution.py:62
  488.2 2.0 convolution_bitcast_fusion.2
  490.2 0.0 all-reduce.3.cloned.1.call-update
  490.2 0.0 copy-done.4
  490.2 1.2 fusion.14
  491.4 1.0 fusion.13
  492.4 256.2 %all-reduce.3.cloned.1.call-done = (f32[256,256]{0,1:T(8,128)}, f32[256,256]{0,1:T(8,128)}) async-done(((f32[256,256]{0,1:T(8,128)}, f32[256,256]{0,1:T(8,128)}), (f32[256,256]{0,1:T(8,128)}, f32[256,256]{0,1:T(8,128)})) %all-reduce.3.cloned.1.call-update) | async-done | bytes 524304 | tf_op jit(solution)/shard_map/psum | solution.py:73
  748.6 1.1 broadcast_multiply_fusion
  749.7 0.8 copy.26
  750.5 0.8 copy.25
  (7 shorter events, 0.0 us)
Async XLA Ops:
  7.2 1.0 copy-start
  7.2 104.8 %all-gather.3.cloned.1.call-start = ((), (), s32[]{:S(2)}) async-start(), calls=%async_computation.2 | async-start | bytes 8650752 | tf_op jit(solution)/shard_map/all_gather | solution.py:25
  10.0 147.5 %reduce-scatter.3.cloned.1.call-start = ((), (), s32[]{:S(2)}) async-start(), calls=%async_computation.3 | async-start | bytes 2359296 | tf_op jit(solution)/shard_map/reduce_scatter | solution.py:43
  112.0 9.5 %copy-start.2 = (bf16[1,1,96,128,128]{4,3,2,1,0:T(8,128)(2,1)S(1)}, bf16[1,1,96,128,128]{4,3,2,1,0:T(8,128)(2,1)}, u32[]{:S(2)}) copy-start(bf16[1,1,96,128,128]{4,3,2,1,0:T(8,128)(2,1)} %param.16) | copy-start | bytes 9437188
  121.5 36.0 %copy-start.5 = (bf16[256,256]{1,0:T(8,128)(2,1)S(1)}, bf16[256,256]{1,0:T(8,128)(2,1)}, u32[]{:S(2)}) copy-start(bf16[256,256]{1,0:T(8,128)(2,1)} %param.11) | copy-start | bytes 393220
  127.0 61.6 %all-gather.5.cloned.1.call-start = ((), (), s32[]{:S(2)}) async-start(), calls=%async_computation.4 | async-start | bytes 2359296 | tf_op jit(solution)/shard_map/all_gather | solution.py:48
  159.8 328.4 %reduce-scatter.5.cloned.1.call-start = ((), (), s32[]{:S(2)}) async-start(), calls=%async_computation.5 | async-start | bytes 8650752 | tf_op jit(solution)/shard_map/reduce_scatter | solution.py:62
  209.2 7.9 %copy-start.6 = (s32[1,1,96]{2,1,0:T(1,128)S(1)}, s32[1,1,96]{2,1,0:T(1,128)}, u32[]{:S(2)}) copy-start(s32[1,1,96]{2,1,0:T(1,128)} %param.14) | copy-start | bytes 1156
  255.1 78.7 %copy-start.3 = (bf16[512,256]{1,0:T(8,128)(2,1)S(1)}, bf16[512,256]{1,0:T(8,128)(2,1)}, u32[]{:S(2)}) copy-start(bf16[512,256]{1,0:T(8,128)(2,1)} %get-tuple-element.21) | copy-start | bytes 786436
  255.1 79.7 %copy-start.1 = (bf16[4096,256]{1,0:T(8,128)(2,1)S(1)}, bf16[4096,256]{1,0:T(8,128)(2,1)}, u32[]{:S(2)}) copy-start(bf16[4096,256]{1,0:T(8,128)(2,1)} %all-gather.5.cloned.1.call-done) | copy-start | bytes 6291460
  255.2 493.4 %all-reduce.3.cloned.1.call-start = ((), (), s32[]{:S(2)}) async-start(), calls=%async_computation.6 | async-start | bytes 1048576 | tf_op jit(solution)/shard_map/psum | solution.py:73
  348.7 141.5 %copy-start.4 = (bf16[256,256]{1,0:T(8,128)(2,1)S(1)}, bf16[256,256]{1,0:T(8,128)(2,1)}, u32[]{:S(2)}) copy-start(bf16[256,256]{1,0:T(8,128)(2,1)} %param.10) | copy-start | bytes 393220
Sparse Core Ops, SparseCore 0:
  11.1 100.8 all-gather.2
  127.1 30.3 reduce-scatter.2
  159.9 28.6 all-gather.4
  255.3 232.8 reduce-scatter.4
  494.2 254.3 all-reduce.2
where the time goes:
time: 758 us
  waiting for transfers between devices  550 us (73%)
  blocking collectives  78.1 us (10%)
  other arithmetic  46.2 us (6%)
  local copies, waits for them, and re-layouts  38.4 us (5%)
  matrix products  30 us (4%)
  between operations  14.5 us (2%)
    psum x1, waiting for transfers between devices, per_device(): lax.psum((local_msg, local_self, local_bias), ('row', 'col'))  256 us
    reduce_scatter x1, waiting for transfers between devices, per_device(): lax.psum_scatter(back_part.astype(jnp.bfloat16), 'row', scatter_dimension...  134 us
    all_gather x1, waiting for transfers between devices, per_device(): column_msgs = lax.all_gather(messages, 'row', axis=0, tiled=True)  101 us
    psum x1, blocking collectives, per_device(): lax.psum((local_msg, local_self, local_bias), ('row', 'col'))  78.1 us
    reduce_scatter x1, waiting for transfers between devices, per_device(): lax.psum_scatter(partial_value.astype(jnp.bfloat16), 'col', scatter_dimen...  30.4 us
    scatter-add x1, other arithmetic, per_device(): jax.ops.segment_sum(backward, slot_cols, num_segments=tile_cols)  29.1 us
    all_gather x1, waiting for transfers between devices, per_device(): grad_rows_all = lax.all_gather(grad_pre, 'col', axis=0, tiled=True)  28.7 us
  transfers between devices with their start and end apart: 5, of which 5 were waited for; matrix products, arithmetic and copies ran while one was open for 3% of the time, Pallas kernels for 0%

commit v1 on v0

--- a/solution.py
+++ b/solution.py
@@ -3,6 +3,13 @@
 import jax.numpy as jnp
 from jax import lax
 from jax.sharding import PartitionSpec as P
+from jax.lax import psum
+
+
+def use_the_routes_all(array_here):
+    for src_i in ("row", "col"):
+        array_here = psum(array_here, src_i)
+    return array_here
 
 
 def activate(pre, row_mask, grad_in):
@@ -70,9 +77,7 @@
     local_msg = jnp.einsum("hf,hg->fg", feats, grad_msg, preferred_element_type=jnp.float32)
     local_self = jnp.einsum("hf,hg->fg", feats, grad_pre, preferred_element_type=jnp.float32)
     local_bias = jnp.sum(grad_pre.astype(jnp.float32), axis=0)
-    total_msg, total_self, total_bias = lax.psum(
-        (local_msg, local_self, local_bias), ("row", "col")
-    )
+    total_msg, total_self, total_bias = use_the_routes_all((local_msg, local_self, local_bias))
     factor = 1.0 / math.sqrt(own_rows * row_count * col_count)
     return (
         hidden,

time: 758 us -> 715 us (0.943)
  waiting for transfers between devices: 550 us -> 497 us
  blocking collectives: 78.1 us -> 86.2 us
    psum x1 -> x2, waiting for transfers between devices: 256 us -> 192 us  [use_the_routes_all(): array_here = psum(array_here, src_i)]
    reduce_scatter x1, waiting for transfers between devices: 134 us -> 145 us  [per_device(): lax.psum_scatter(back_part.astype(jnp.bfloat16), 'row', scatter_dimension...]
    psum x1 -> x2, blocking collectives: 78.1 us -> 86.2 us  [use_the_routes_all(): array_here = psum(array_here, src_i)]
  transfers between devices with their start and end apart: 5 -> 6, of which waited for: 5 -> 6; matrix products, arithmetic and copies ran while one was open for 3% -> 3% of each run, Pallas kernels for 0% -> 0%
where the time goes in v1:
time: 715 us; the launch traced here: 712 us
  waiting for transfers between devices  497 us (70%)
  blocking collectives  86.2 us (12%)
  other arithmetic  46.2 us (6%)
  local copies, waits for them, and re-layouts  38.4 us (5%)
  matrix products  29.1 us (4%)
  between operations  14.8 us (2%)
    psum x2, waiting for transfers between devices, use_the_routes_all(): array_here = psum(array_here, src_i)  192 us
    reduce_scatter x1, waiting for transfers between devices, per_device(): lax.psum_scatter(back_part.astype(jnp.bfloat16), 'row', scatter_dimension...  145 us
    all_gather x1, waiting for transfers between devices, per_device(): column_msgs = lax.all_gather(messages, 'row', axis=0, tiled=True)  101 us
    psum x2, blocking collectives, use_the_routes_all(): array_here = psum(array_here, src_i)  86.2 us
    reduce_scatter x1, waiting for transfers between devices, per_device(): lax.psum_scatter(partial_value.astype(jnp.bfloat16), 'col', scatter_dimen...  30.4 us
    scatter-add x1, other arithmetic, per_device(): jax.ops.segment_sum(backward, slot_cols, num_segments=tile_cols)  29.1 us
    all_gather x1, waiting for transfers between devices, per_device(): grad_rows_all = lax.all_gather(grad_pre, 'col', axis=0, tiled=True)  28.7 us
  transfers between devices with their start and end apart: 6, of which 6 were waited for; matrix products, arithmetic and copies ran while one was open for 3% of the time, Pallas kernels for 0%

profile of v1, /device:TPU:2, one launch (start us, length us, event | category | flops | bytes accessed | tf_op | source)
XLA Modules:
  0.0 712.2 jit_solution(14234278752085636237)
XLA Ops:
  7.2 0.0 copy-start
  7.2 0.0 all-gather.3.cloned.1.call-start
  7.2 0.7 convert_element_type.67
  7.9 0.2 copy-done
  8.1 1.8 fusion.12
  10.0 0.0 all-gather.3.cloned.1.call-update
  10.0 0.0 reduce-scatter.3.cloned.1.call-start
  10.7 0.7 fusion.16
  11.4 100.7 %all-gather.3.cloned.1.call-done = bf16[16384,256]{1,0:T(8,128)(2,1)} async-done(((bf16[512,256]{1,0:T(8,128)(2,1)}), bf16[16384,256]{1,0:T(8,128)(2,1)}) %all-gather.3.cloned.1.call-update) | async-done | bytes 8388624 | tf_op jit(solution)/shard_map/all_gather | solution.py:32
  112.0 9.5 %gather_fusion = bf16[96,128,256]{2,1,0:T(8,128)(2,1)} fusion(bf16[128,128,256]{2,1,0:T(8,128)(2,1)} %bitcast.53, s32[1024]{0:T(1024)S(1)} %pad_clamp_fusion), kind=kCustom, calls=%fused_computation | custom fusion | bytes 12583296 | tf_op jit(solution)/shard_map/gather | solution.py:44
  121.5 0.0 copy-done.2
  121.5 5.5 bitcast_convert_fusion
  127.0 0.0 reduce-scatter.3.cloned.1.call-update
  127.0 0.0 all-gather.5.cloned.1.call-start
  127.1 30.4 %reduce-scatter.3.cloned.1.call-done = bf16[512,256]{1,0:T(8,128)(2,1)} async-done(((bf16[4096,256]{1,0:T(8,128)(2,1)}), bf16[512,256]{1,0:T(8,128)(2,1)}) %reduce-scatter.3.cloned.1.call-update) | async-done | bytes 262160 | tf_op jit(solution)/shard_map/reduce_scatter | solution.py:50
  157.5 0.0 copy-done.6
  157.5 2.3 convert_reduce_fusion
  159.8 0.0 all-gather.5.cloned.1.call-update
  159.8 0.0 reduce-scatter.5.cloned.1.call-start
  159.9 28.7 %all-gather.5.cloned.1.call-done = bf16[4096,256]{1,0:T(8,128)(2,1)} async-done(((bf16[512,256]{1,0:T(8,128)(2,1)}), bf16[4096,256]{1,0:T(8,128)(2,1)}) %all-gather.5.cloned.1.call-update) | async-done | bytes 2097168 | tf_op jit(solution)/shard_map/all_gather | solution.py:55
  188.6 8.0 %convolution_bitcast_fusion = f32[3,32,128,256]{2,3,0,1:T(8,128)} fusion(bf16[32,128,256,1]{2,1,3,0:T(8,128)(2,1)} %bitcast.51, bf16[3,32,128,128]{3,2,1,0:T(8,128)(2,1)S(1)} %bitcast.55, bf16[3,32]{0,1:T(8,128)(2,1)S(1)} %fusion.15), kind=kOutput, calls=%fused_computation.7 | convolution fusion | flops 811597824 | bytes 17825984 | tf_op jit(solution)/shard_map/krij,rif->krjf/dot_general | solution.py:57
  196.6 12.6 %copy.22 = f32[3,32,128,256]{3,2,1,0:T(8,128)} copy(f32[3,32,128,256]{2,3,0,1:T(8,128)} %convolution_bitcast_fusion) | data formatting | bytes 25165824 | tf_op jit(solution)/shard_map/krij,rif->krjf/transpose | solution.py:57
  209.2 7.8 %broadcast_in_dim.2 = f32[128,128,256]{2,1,0:T(8,128)} broadcast(f32[]{:T(128)} %constant.4.clone.1), dimensions={} | broadcast | bytes 16777220 | tf_op jit(solution)/shard_map/broadcast_in_dim | solution.py:60
  217.0 0.0 copy-done.7
  217.0 29.1 %scatter_fusion = f32[128,128,256]{2,1,0:T(8,128)} fusion(f32[128,128,256]{2,1,0:T(8,128)} %broadcast_in_dim.2, s32[96]{0:T(128)S(1)} %bitcast.57, f32[96,128,256]{2,1,0:T(8,128)} %bitcast.46), kind=kCustom, calls=%fused_computation.1 | custom fusion | flops 3145728 | bytes 37749120 | tf_op jit(solution)/shard_map/scatter-add | solution.py:60
  246.1 9.0 %convert_element_type.75 = bf16[128,128,256]{2,1,0:T(8,128)(2,1)} convert(f32[128,128,256]{2,1,0:T(8,128)} %scatter_fusion) | non-fusion elementwise | flops 4194304 | bytes 25165824 | tf_op jit(solution)/shard_map/convert_element_type | solution.py:70
  255.1 0.0 reduce-scatter.5.cloned.1.call-update
  255.2 0.0 all-reduce.5.cloned.1.call-start
  255.2 75.4 %psum.46 = f32[256]{0:T(256)S(1)} all-reduce(f32[256]{0:T(256)S(1)} %get-tuple-element.22), channel_id=1, replica_groups=mesh['row'=32,'col'=8] {'row'}, use_global_device_ids=true, to_apply=%region_8.0 | all-reduce | flops 256 | bytes 2048 | tf_op jit(solution)/shard_map/psum | solution.py:11
  330.7 10.8 %psum.47 = f32[256]{0:T(256)S(1)} all-reduce(f32[256]{0:T(256)S(1)} %psum.46), channel_id=1, replica_groups=mesh['row'=32,'col'=8] {'col'}, use_global_device_ids=true, to_apply=%region_9.0 | all-reduce | flops 256 | bytes 2048 | tf_op jit(solution)/shard_map/psum | solution.py:11
  341.4 0.6 broadcast_multiply_fusion.2
  342.0 0.0 copy-done.3
  342.0 1.0 convolution_bitcast_fusion.1
  343.0 145.1 %reduce-scatter.5.cloned.1.call-done = bf16[512,256]{1,0:T(8,128)(2,1)} async-done(((bf16[16384,256]{1,0:T(8,128)(2,1)}), bf16[512,256]{1,0:T(8,128)(2,1)}) %reduce-scatter.5.cloned.1.call-update) | async-done | bytes 262160 | tf_op jit(solution)/shard_map/reduce_scatter | solution.py:69
  488.1 2.0 convolution_bitcast_fusion.2
  490.1 0.0 all-reduce.5.cloned.1.call-update
  490.1 0.2 all-reduce.7.cloned.1.call-start
  490.4 7.3 %fusion.4 = f32[3,32,128,128]{2,3,0,1:T(8,128)} fusion(bf16[32,128,256,1]{2,1,3,0:T(8,128)(2,1)S(1)} %bitcast.52, bf16[3,32,128,256]{3,2,1,0:T(8,128)(2,1)} %bitcast.49), kind=kOutput, calls=%fused_computation.10 | convolution fusion | flops 805306368 | bytes 14680064 | tf_op jit(solution)/shard_map/rif,krjf->krij/dot_general | solution.py:64
  497.6 6.6 copy.24
  504.2 5.1 multiply_convert_fusion
  509.3 130.0 %all-reduce.5.cloned.1.call-done = (f32[256,256]{0,1:T(8,128)}, f32[256,256]{0,1:T(8,128)}) async-done(((f32[256,256]{0,1:T(8,128)}, f32[256,256]{0,1:T(8,128)}), (f32[256,256]{0,1:T(8,128)}, f32[256,256]{0,1:T(8,128)})) %all-reduce.5.cloned.1.call-update) | async-done | bytes 524304 | tf_op jit(solution)/shard_map/psum | solution.py:11
  639.3 0.0 all-reduce.7.cloned.1.call-update
  639.3 0.3 fusion.14
  639.6 1.0 fusion.13
  640.6 62.0 %all-reduce.7.cloned.1.call-done = (f32[256,256]{0,1:T(8,128)}, f32[256,256]{0,1:T(8,128)}) async-done(((f32[256,256]{0,1:T(8,128)}, f32[256,256]{0,1:T(8,128)}), (f32[256,256]{0,1:T(8,128)}, f32[256,256]{0,1:T(8,128)})) %all-reduce.7.cloned.1.call-update) | async-done | bytes 524304 | tf_op jit(solution)/shard_map/psum | solution.py:11
  702.6 1.1 broadcast_multiply_fusion
  703.7 0.8 copy.26
  704.5 0.8 copy.25
  (13 shorter events, 0.0 us)
Async XLA Ops:
  7.2 1.0 copy-start
  7.2 104.8 %all-gather.3.cloned.1.call-start = ((), (), s32[]{:S(2)}) async-start(), calls=%async_computation.2 | async-start | bytes 8650752 | tf_op jit(solution)/shard_map/all_gather | solution.py:32
  10.0 147.5 %reduce-scatter.3.cloned.1.call-start = ((), (), s32[]{:S(2)}) async-start(), calls=%async_computation.3 | async-start | bytes 2359296 | tf_op jit(solution)/shard_map/reduce_scatter | solution.py:50
  112.0 9.5 %copy-start.2 = (bf16[1,1,96,128,128]{4,3,2,1,0:T(8,128)(2,1)S(1)}, bf16[1,1,96,128,128]{4,3,2,1,0:T(8,128)(2,1)}, u32[]{:S(2)}) copy-start(bf16[1,1,96,128,128]{4,3,2,1,0:T(8,128)(2,1)} %param.16) | copy-start | bytes 9437188
  121.5 36.0 %copy-start.6 = (bf16[256,256]{1,0:T(8,128)(2,1)S(1)}, bf16[256,256]{1,0:T(8,128)(2,1)}, u32[]{:S(2)}) copy-start(bf16[256,256]{1,0:T(8,128)(2,1)} %param.11) | copy-start | bytes 393220
  127.0 61.6 %all-gather.5.cloned.1.call-start = ((), (), s32[]{:S(2)}) async-start(), calls=%async_computation.4 | async-start | bytes 2359296 | tf_op jit(solution)/shard_map/all_gather | solution.py:55
  159.8 328.3 %reduce-scatter.5.cloned.1.call-start = ((), (), s32[]{:S(2)}) async-start(), calls=%async_computation.5 | async-start | bytes 8650752 | tf_op jit(solution)/shard_map/reduce_scatter | solution.py:69
  209.2 7.9 %copy-start.7 = (s32[1,1,96]{2,1,0:T(1,128)S(1)}, s32[1,1,96]{2,1,0:T(1,128)}, u32[]{:S(2)}) copy-start(s32[1,1,96]{2,1,0:T(1,128)} %param.14) | copy-start | bytes 1156
  255.1 86.9 %copy-start.3 = (bf16[512,256]{1,0:T(8,128)(2,1)S(1)}, bf16[512,256]{1,0:T(8,128)(2,1)}, u32[]{:S(2)}) copy-start(bf16[512,256]{1,0:T(8,128)(2,1)} %get-tuple-element.23) | copy-start | bytes 786436
  255.1 235.2 %copy-start.1 = (bf16[4096,256]{1,0:T(8,128)(2,1)S(1)}, bf16[4096,256]{1,0:T(8,128)(2,1)}, u32[]{:S(2)}) copy-start(bf16[4096,256]{1,0:T(8,128)(2,1)} %all-gather.5.cloned.1.call-done) | copy-start | bytes 6291460
  255.2 384.1 %all-reduce.5.cloned.1.call-start = ((), (), s32[]{:S(2)}) async-start(), calls=%async_computation.6 | async-start | bytes 1048576 | tf_op jit(solution)/shard_map/psum | solution.py:11
  490.1 212.5 %all-reduce.7.cloned.1.call-start = ((), (), s32[]{:S(2)}) async-start(), calls=%async_computation.7 | async-start | bytes 1048576 | tf_op jit(solution)/shard_map/psum | solution.py:11
  504.2 135.1 %copy-start.4 = (bf16[512,256]{1,0:T(8,128)(2,1)S(1)}, bf16[512,256]{1,0:T(8,128)(2,1)}, u32[]{:S(2)}) copy-start(bf16[512,256]{1,0:T(8,128)(2,1)} %reduce-scatter.5.cloned.1.call-done) | copy-start | bytes 786436
  504.2 135.1 %copy-start.5 = (bf16[256,256]{1,0:T(8,128)(2,1)S(1)}, bf16[256,256]{1,0:T(8,128)(2,1)}, u32[]{:S(2)}) copy-start(bf16[256,256]{1,0:T(8,128)(2,1)} %param.10) | copy-start | bytes 393220
Sparse Core Ops, SparseCore 0:
  11.1 100.8 all-gather.2
  127.1 30.3 reduce-scatter.2
  159.9 28.6 all-gather.4
  255.3 232.7 reduce-scatter.4
  491.9 147.2 all-reduce.4
  641.5 61.0 all-reduce.6
